TPU v7x, 512 devices: a whole 4x8x8 slice. The times are simulated.
512 devices in a mesh: aisle: 32 (over z_hi, y), span: 16 (over x, z_lo, core).
Axes of the slice: x: 4, y: 8, z: 8 (z_hi: 4, z_lo: 2; z = z_hi * 2 + z_lo), core: 2. Of those that a mesh axis runs over, the one named last changes fastest.
Arguments:
- downflow_motion: float32 [512, 512, 256], P('aisle', 'span'), may hold values from -6 to 6
- crossflow_motion: float32 [512, 512, 256], P('aisle', 'span'), may hold values from -6 to 6
- upright_motion: float32 [512, 512, 256], P('aisle', 'span'), may hold values from -6 to 6
- thermal_anomaly: float32 [512, 512, 256], P('aisle', 'span'), may hold values from -6 to 6
- height_to_eigenbasis: float32 [256, 256], replicated, may hold values from -1 to 2
- eigenbasis_to_height: float32 [256, 256], replicated, may hold values from -1 to 2
- negated_height_spectrum: float32 [256], replicated, may hold values from 0.002 to 0.02
Outputs:
- east_after: float32 [512, 512, 256], P('aisle', 'span')
- north_after: float32 [512, 512, 256], P('aisle', 'span')
- upward_after: float32 [512, 512, 256], P('aisle', 'span')
- heat_after: float32 [512, 512, 256], P('aisle', 'span')
All inputs are finite; a program needn't handle non-finite values.
Results may differ from a plain program's by a relative error of at most 0.0003.
Values sent between devices are 32-bit elements; how exact they have to be, the bound alone decides.
No kernel may reach another device: no remote copies, remote signals or barrier semaphores. Data moves between devices by JAX's collectives and lax.ppermute only.
A program may use at most 128 MiB of HBM per device.

v0:
```python
import functools
import math

import jax
import jax.numpy as jnp
import ml_dtypes
import numpy as np
from jax import lax
from jax.experimental import pallas as pl
from jax.experimental.pallas import tpu as pltpu
from jax.sharding import PartitionSpec as P

f32 = jnp.float32
bf16 = jnp.bfloat16
step_gain = 0.1 * 8.0 / 15.0
viscosity = 0.01
smagorinsky = 0.05
prandtl = 0.7
buoyancy = 1.0
strain_floor = 0.25

AISLE = 32
SPAN = 16
BX = 16
BY = 32
NZ = 256
NY = SPAN * BY
KS = NZ // SPAN
HALF = NY // 2
XR = BX + 1
ROWS = 72


def y_tables():
    cells = np.arange(HALF)
    even = [(m, 0) for m in range(0, HALF + 1, 2)] + [(m, 1) for m in range(2, HALF, 2)]
    odd = [(m, 0) for m in range(1, HALF, 2)] + [(m, 1) for m in range(1, HALF, 2)]
    modes = even + odd
    edges = (BY * (np.arange(SPAN) + 1)) % NY

    def rows(at):
        wave = np.array([m for m, _ in modes])
        odd_part = np.array([s for _, s in modes])
        angle = 2.0 * np.pi / NY * ((at[:, None] * wave[None, :]) % NY)
        return np.where(odd_part[None, :] == 1, np.sin(angle), np.cos(angle))

    main = rows(cells)
    extra = np.zeros((128, NY))
    extra[32 : 32 + SPAN] = rows(edges)
    table = np.concatenate([main, extra], axis=0).astype(np.float32)
    high = table.astype(ml_dtypes.bfloat16)
    low = (table - high.astype(np.float32)).astype(ml_dtypes.bfloat16)
    wave = np.array([m for m, _ in modes])
    eigen = (4.0 * np.sin(np.pi * wave / NY) ** 2).astype(np.float32)
    weight = np.where((wave == 0) | (wave == HALF), 1.0 / NY, 2.0 / NY).astype(np.float32)
    return high, low, eigen, weight


TABLE_HIGH, TABLE_LOW, EIGEN, WEIGHT = y_tables()


def split(value):
    high = value.astype(bf16)
    low = (value - high.astype(f32)).astype(bf16)
    return high, low


def dot3(a, b, dims):
    def one(p, q):
        return lax.dot_general(p, q, (dims, ((), ())), preferred_element_type=f32)

    return one(a[0], b[0]) + (one(a[0], b[1]) + one(a[1], b[0]))


NN = ((1,), (0,))
NT = ((1,), (1,))


def exchange(vectors, unit, lane):
    vectors = list(vectors)
    distance = len(vectors) // 2
    while distance:
        upper = (lane // (unit * distance)) % 2 == 1
        for i in range(len(vectors)):
            if i & distance:
                continue
            a, b = vectors[i], vectors[i + distance]
            vectors[i] = jnp.where(upper, pltpu.roll(b, unit * distance, 1), a)
            vectors[i + distance] = jnp.where(upper, b, pltpu.roll(a, 128 - unit * distance, 1))
        distance //= 2
    return vectors


def pack_kernel(*refs):
    x_first, x_last, y_first, y_last = refs[16:]
    for f in range(4):
        x_first[f] = refs[f][0]
        x_last[f] = refs[4 + f][0]
        y_first[f] = refs[8 + f][:, 0, :]
        y_last[f] = refs[12 + f][:, 7, :]


def pack(fields):
    plane = lambda at: pl.BlockSpec((1, BY, NZ), lambda i: (at, 0, 0))
    rows = lambda at: pl.BlockSpec((BX, 8, NZ), lambda i: (0, at, 0))
    whole = lambda shape: pl.BlockSpec(shape, lambda i: (0, 0, 0))
    xs, ys = (4, BY, NZ), (4, BX, NZ)
    return pl.pallas_call(
        pack_kernel,
        grid=(1,),
        in_specs=[plane(0)] * 4 + [plane(BX - 1)] * 4 + [rows(0)] * 4 + [rows(BY // 8 - 1)] * 4,
        out_specs=[whole(xs), whole(xs), whole(ys), whole(ys)],
        out_shape=[jax.ShapeDtypeStruct(s, f32) for s in (xs, xs, ys, ys)],
        name="pack",
    )(*fields, *fields, *fields, *fields)


def predict_kernel(
    fd, fc, fu, ft, xlo, xhi, ylo, yhi, basis, es, ns, us, ts, chunk, buf, src, sems
):
    copies = [pltpu.make_async_copy(f, buf.at[i, pl.ds(1, BX)], sems.at[i]) for i, f in enumerate((fd, fc, fu, ft))]
    copies.append(pltpu.make_async_copy(xlo, buf.at[:, 0], sems.at[4]))
    copies.append(pltpu.make_async_copy(xhi, buf.at[:, BX + 1], sems.at[5]))
    for copy in copies:
        copy.start()
    row = lax.broadcasted_iota(jnp.int32, (BY, NZ), 0)
    lane = lax.broadcasted_iota(jnp.int32, (BY, NZ), 1)
    base = BX * BY
    src[base + BY :, :] = jnp.zeros((128 - BY, NZ), f32)
    for copy in copies:
        copy.wait()
    zero = jnp.zeros((BY, NZ), f32)

    def south_of(value, edge):
        return jnp.where(row == 0, edge, pltpu.roll(value, 1, 0))

    def lower_of(value):
        return jnp.where(lane == 0, 0.0, pltpu.roll(value, 1, 1))

    def plane(x, east_prev):
        centre, steps, laplace = [], [], []
        for f in range(4):
            c = buf[f, x + 1]
            w, e = buf[f, x], buf[f, x + 2]
            s = south_of(c, ylo[f, pl.ds(x, 1), :])
            n = jnp.where(row == BY - 1, yhi[f, pl.ds(x, 1), :], pltpu.roll(c, BY - 1, 0))
            l = lower_of(c)
            u = jnp.where(lane == NZ - 1, 0.0, pltpu.roll(c, NZ - 1, 1))
            centre.append(c)
            steps.append((e - w, n - s, u - l))
            laplace.append((e + w) + (n + s) + (u + l) - 6.0 * c)
        strain = sum(d * d for f in range(3) for d in steps[f])
        turbulent = viscosity + smagorinsky * jnp.sqrt(0.25 * strain + strain_floor)
        stars = []
        for f in range(4):
            k = turbulent if f < 3 else turbulent * (1.0 / prandtl)
            dx, dy, dz = steps[f]
            transport = 0.5 * (centre[0] * dx + centre[1] * dy + centre[2] * dz)
            tendency = k * laplace[f] - transport
            if f == 2:
                tendency = tendency + buoyancy * centre[3]
            stars.append(centre[f] + step_gain * tendency)
        east, north, upward, heat = stars
        es[x] = east
        ns[x] = north
        us[x] = upward
        ts[x] = heat
        flux = (east - east_prev) + (north - south_of(north, zero)) + (upward - lower_of(upward))
        src[pl.ds(pl.multiple_of(x * BY, BY), BY), :] = flux
        src[pl.ds(base + BY + x, 1), :] = -north[BY - 1 :, :]
        return east

    last = lax.fori_loop(0, BX, plane, zero)
    src[base : base + BY, :] = -last
    forward = split(basis[...])
    for t in range(5):
        modes = dot3(forward, split(src[t * 128 : (t + 1) * 128, :]), NT)
        if t < 4:
            chunk[:, t * KS : (t + 1) * KS, :] = modes.reshape(SPAN, KS, 128)
        else:
            modes = modes.reshape(SPAN, 2, 8, 128)
            lanes = lax.broadcasted_iota(jnp.int32, (8, 128), 1)
            for s in range(SPAN):
                chunk[s, 4 * KS :, :] = jnp.where(lanes < 64, modes[s, 0], pltpu.roll(modes[s, 1], 64, 1))


def predict(fields, xlo, xhi, ylo, yhi, basis):
    any_spec = pl.BlockSpec(memory_space=pl.ANY)
    vmem = pl.BlockSpec(memory_space=pltpu.VMEM)
    block = jax.ShapeDtypeStruct((BX, BY, NZ), f32)
    return pl.pallas_call(
        predict_kernel,
        in_specs=[any_spec] * 6 + [vmem] * 3,
        out_specs=[vmem] * 5,
        out_shape=[block] * 4 + [jax.ShapeDtypeStruct((SPAN, ROWS, 128), f32)],
        scratch_shapes=[
            pltpu.VMEM((4, BX + 2, BY, NZ), f32),
            pltpu.VMEM((BX * BY + 128, NZ), f32),
            pltpu.SemaphoreType.DMA((6,)),
        ],
        name="predict",
    )(*fields, xlo, xhi, ylo, yhi, basis)


def decay(mu):
    root = jnp.sqrt(mu + 0.25 * mu * mu)
    return root, 1.0 / (1.0 + 0.5 * mu + root)


def transform_kernel(recv, mu, high, low, local, sums, work, extra):
    lane16 = lax.broadcasted_iota(jnp.int32, (KS, 128), 1)
    lane8 = lax.broadcasted_iota(jnp.int32, (8, 128), 1)
    for t in range(4):
        for group in range(4):
            pieces = [recv[4 * group + c, t * KS : (t + 1) * KS, :] for c in range(4)]
            for i, piece in enumerate(exchange(pieces, 32, lane16)):
                x = 4 * t + i
                work[x * KS : (x + 1) * KS, group * 128 : (group + 1) * 128] = piece
    extras = [recv[c, 4 * KS :, :] for c in range(SPAN)]
    for kt in range(2):
        for group in range(4):
            total = None
            for c in range(4):
                piece = pltpu.roll(extras[4 * group + c], (32 * c - 64 * kt) % 128, 1) if (32 * c - 64 * kt) % 128 else extras[4 * group + c]
                total = piece if total is None else jnp.where(lane8 // 32 == c, piece, total)
            at = BX * KS + kt * 8
            work[at : at + 8, group * 128 : (group + 1) * 128] = total
    for x, piece in enumerate(exchange(extras, 1, lane8)):
        extra[x * KS : x * KS + 8, :] = piece
        extra[x * KS + 8 : (x + 1) * KS, :] = pltpu.roll(piece, 64, 1)
    extra[BX * KS :, :] = jnp.zeros((KS, 128), f32)
    lower, upper = work[:, :HALF], work[:, HALF:]
    beyond = split(extra[...])
    for part in range(2):
        columns = slice(part * HALF, (part + 1) * HALF)
        folded = split(lower - upper if part else lower + upper)
        main = dot3(folded, (high[:HALF, columns], low[:HALF, columns]), NN)
        rest = dot3(beyond, (high[HALF:, columns], low[HALF:, columns]), NN)
        work[:, columns] = main + rest
    _, ratio = decay(mu[...])
    state = None
    for x in range(XR):
        value = work[x * KS : (x + 1) * KS, :]
        if state is not None:
            local[x * KS : (x + 1) * KS, :] = ratio * state
            state = value + ratio * state
        else:
            local[:KS, :] = jnp.zeros((KS, NY), f32)
            state = value
    ahead = None
    for x in range(XR - 1, -1, -1):
        value = work[x * KS : (x + 1) * KS, :]
        ahead = value if ahead is None else value + ratio * ahead
        local[x * KS : (x + 1) * KS, :] += ahead
    for kind, value in enumerate((state, ahead)):
        for kt in range(4):
            for mt in range(4):
                sums[kind * 16 + kt * 4 + mt] = value[4 * kt : 4 * kt + 4, 128 * mt : 128 * (mt + 1)]


def transform(recv, mu, high, low):
    vmem = pl.BlockSpec(memory_space=pltpu.VMEM)
    return pl.pallas_call(
        transform_kernel,
        in_specs=[vmem] * 4,
        out_specs=[vmem] * 2,
        out_shape=[
            jax.ShapeDtypeStruct((XR * KS, NY), f32),
            jax.ShapeDtypeStruct((AISLE, 4, 128), f32),
        ],
        scratch_shapes=[pltpu.VMEM((XR * KS, NY), f32), pltpu.VMEM((XR * KS, 128), f32)],
        name="transform",
    )(recv, mu, high, low)


def carry_kernel(kind, sums, mu, carries):
    backwards = kind[0]
    _, ratio = decay(mu[...])
    step = ratio
    for _ in range(4):
        step = step * step
    around = step
    for _ in range(5):
        around = around * around

    def place(i):
        return i + backwards * (AISLE - 1 - 2 * i)

    def gather(i, state):
        return sums[place(i)] + step * state

    state = lax.fori_loop(0, AISLE, gather, jnp.zeros_like(step), unroll=8) / (1.0 - around)

    def spread(i, state):
        at = place(i)
        carries[at] = state
        return sums[at] + step * state

    lax.fori_loop(0, AISLE, spread, state, unroll=8)


def carry(kind, sums, mu):
    vmem = pl.BlockSpec(memory_space=pltpu.VMEM)
    return pl.pallas_call(
        carry_kernel,
        in_specs=[pl.BlockSpec(memory_space=pltpu.SMEM), vmem, vmem],
        out_specs=vmem,
        out_shape=jax.ShapeDtypeStruct((AISLE, 4, 128), f32),
        name="carry",
    )(kind, sums, mu)


def inverse_kernel(local, carries, mu, weight, high, low, chunk, ends, work_high, work_low, work, extra):
    lane16 = lax.broadcasted_iota(jnp.int32, (KS, 128), 1)
    lane8 = lax.broadcasted_iota(jnp.int32, (8, 128), 1)
    for kind in range(2):
        for kt in range(4):
            for mt in range(4):
                ends[kind, 4 * kt : 4 * kt + 4, 128 * mt : 128 * (mt + 1)] = carries[kind * 16 + kt * 4 + mt]
    root, ratio = decay(mu[...])
    scale = -0.5 * weight[...] / root
    powers = [jnp.ones_like(ratio)]
    behind, ahead = ends[0], ends[1]
    backs = [ahead]
    for x in range(BX):
        backs.append(ratio * backs[-1])
    for x in range(XR):
        rows = slice(x * KS, (x + 1) * KS)
        value = split(scale * (local[rows, :] + behind + backs[BX - x]))
        work_high[rows, :] = value[0]
        work_low[rows, :] = value[1]
        behind = ratio * behind
    parts = []
    for part in range(2):
        columns = slice(part * HALF, (part + 1) * HALF)
        value = (work_high[:, columns], work_low[:, columns])
        parts.append(
            (
                dot3(value, (high[:HALF, columns], low[:HALF, columns]), NT),
                dot3(value, (high[HALF:, columns], low[HALF:, columns]), NT),
            )
        )
    work[:, :HALF] = parts[0][0] + parts[1][0]
    work[:, HALF:] = parts[0][0] - parts[1][0]
    extra[...] = parts[0][1] + parts[1][1]
    for t in range(4):
        for group in range(4):
            pieces = [work[x * KS : (x + 1) * KS, group * 128 : (group + 1) * 128] for x in range(4 * t, 4 * t + 4)]
            for i, piece in enumerate(exchange(pieces, 32, lane16)):
                chunk[4 * group + i, t * KS : (t + 1) * KS, :] = piece
    edges = []
    for x in range(BX):
        edges.append(
            jnp.where(lane8 < 64, extra[x * KS : x * KS + 8, :], pltpu.roll(extra[x * KS + 8 : (x + 1) * KS, :], 64, 1))
        )
    for c, piece in enumerate(exchange(edges, 1, lane8)):
        group, i = divmod(c, 4)
        for kt in range(2):
            at = BX * KS + kt * 8
            last = work[at : at + 8, group * 128 : (group + 1) * 128]
            turn = (64 * kt - 32 * i) % 128
            last = pltpu.roll(last, turn, 1) if turn else last
            piece = jnp.where(lane8 // 32 == 2 * kt, last, piece)
        chunk[c, 4 * KS :, :] = piece


def inverse(local, carries, mu, weight, high, low):
    vmem = pl.BlockSpec(memory_space=pltpu.VMEM)
    return pl.pallas_call(
        inverse_kernel,
        in_specs=[vmem] * 6,
        out_specs=vmem,
        out_shape=jax.ShapeDtypeStruct((SPAN, ROWS, 128), f32),
        scratch_shapes=[
            pltpu.VMEM((2, KS, NY), f32),
            pltpu.VMEM((XR * KS, NY), bf16),
            pltpu.VMEM((XR * KS, NY), bf16),
            pltpu.VMEM((XR * KS, NY), f32),
            pltpu.VMEM((XR * KS, 128), f32),
        ],
        name="inverse",
    )(local, carries, mu, weight, high, low)


def correct_kernel(recv, basis, es, ns, us, east, north, upward, press):
    back = split(basis[...])
    for t in range(4):
        modes = split(recv[:, t * KS : (t + 1) * KS, :].reshape(NZ, 128))
        press[t * 128 : (t + 1) * 128, :] = dot3(back, modes, NN).T
    extras = []
    for s in range(SPAN):
        piece = recv[s, 4 * KS :, :]
        extras.append(piece)
        extras.append(pltpu.roll(piece, 64, 1))
    modes = split(jnp.concatenate(extras, axis=0))
    press[512:640, :] = dot3(back, modes, NN).T
    row = lax.broadcasted_iota(jnp.int32, (BY, NZ), 0)
    lane = lax.broadcasted_iota(jnp.int32, (BY, NZ), 1)

    def plane(x, here):
        beyond = press[pl.ds(pl.multiple_of((x + 1) * BY, BY), BY), :]
        edge = press[pl.ds(BX * BY + BY + x, 1), :]
        beside = jnp.where(row == BY - 1, edge, pltpu.roll(here, BY - 1, 0))
        above = jnp.where(lane == NZ - 1, 0.0, pltpu.roll(here, NZ - 1, 1))
        east[x] = es[x] - (beyond - here)
        north[x] = ns[x] - (beside - here)
        upward[x] = us[x] - (above - here)
        return beyond

    lax.fori_loop(0, BX, plane, press[:BY, :])


def correct(recv, basis, es, ns, us):
    vmem = pl.BlockSpec(memory_space=pltpu.VMEM)
    block = jax.ShapeDtypeStruct((BX, BY, NZ), f32)
    return pl.pallas_call(
        correct_kernel,
        in_specs=[vmem] * 5,
        out_specs=[vmem] * 3,
        out_shape=[block] * 3,
        scratch_shapes=[pltpu.VMEM((BX * BY + 128, NZ), f32)],
        name="correct",
    )(recv, basis, es, ns, us)


def ring(axis, count, step, value):
    return lax.ppermute(value, axis, [(i, (i + step) % count) for i in range(count)])


def per_device(
    downflow_motion,
    crossflow_motion,
    upright_motion,
    thermal_anomaly,
    height_to_eigenbasis,
    eigenbasis_to_height,
    negated_height_spectrum,
):
    fields = (downflow_motion, crossflow_motion, upright_motion, thermal_anomaly)
    x_first, x_last, y_first, y_last = pack(fields)
    xlo = ring("aisle", AISLE, 1, x_last)
    xhi = ring("aisle", AISLE, -1, x_first)
    ylo = ring("span", SPAN, 1, y_last)
    yhi = ring("span", SPAN, -1, y_first)
    share = lax.dynamic_slice(negated_height_spectrum, (lax.axis_index("span") * KS,), (KS,))
    mu = share[:, None] + jnp.asarray(EIGEN)[None, :]
    turn = lax.axis_index("aisle")
    mu_lines = lax.dynamic_slice(mu, ((turn // 4) % 4 * 4, turn % 4 * 128), (4, 128))
    kind = (turn // 16).astype(jnp.int32).reshape(1)
    high, low = jnp.asarray(TABLE_HIGH), jnp.asarray(TABLE_LOW)
    weight = jnp.asarray(WEIGHT).reshape(1, NY)
    swap = functools.partial(lax.all_to_all, split_axis=0, concat_axis=0, tiled=True)
    es, ns, us, heat, chunk = predict(fields, xlo, xhi, ylo, yhi, height_to_eigenbasis)
    local, sums = transform(swap(chunk, "span"), mu, high, low)
    carries = carry(kind, swap(sums, "aisle"), mu_lines)
    chunk = inverse(local, swap(carries, "aisle"), mu, weight, high, low)
    east, north, upward = correct(swap(chunk, "span"), eigenbasis_to_height, es, ns, us)
    return (east, north, upward, heat)


def solution(mesh):
    block = P("aisle", "span", None)
    return jax.shard_map(
        per_device,
        mesh=mesh,
        in_specs=(block,) * 4 + (P(), P(), P()),
        out_specs=(block,) * 4,
        check_vma=False,
    )
```

profile of v0, /device:TPU:1, one launch (start us, length us, event | category | flops | bytes accessed | tf_op | source)
XLA Modules:
  0.0 122.7 jit_solution(4696138591659492224)
XLA Ops:
  0.6 2.2 %pack.1 = (f32[4,32,256]{2,1,0:T(8,128)}, f32[4,32,256]{2,1,0:T(8,128)}, f32[4,16,256]{2,1,0:T(8,128)}, f32[4,16,256]{2,1,0:T(8,128)}) custom-call(f32[16,32,256]{2,1,0:T(8,128)} %fd.1, f32[16,32,256]{2,1,0:T(8,128)} %fc.1, f32[16,32,256]{2,1,0:T(8,128)} %fu.1, f32[16,32,256]{2,1,0:T(8,128)} %ft.1, f32[16,32,256]{2,1,0:T(8,128)} %fd.1, f32[16,32,256]{2,1,0:T(8,128)} %fc.1, ...), custom_call_target="tpu_custom_call" | custom-call | tf_op jit(solution)/shard_map/pack/pallas_call | solution.py:108
  2.8 4.0 %collective-permute-start = (f32[4,32,256]{2,1,0:T(8,128)}, f32[4,32,256]{2,1,0:T(8,128)S(1)}, u32[]{:S(2)}, u32[]{:S(2)}) collective-permute-start(f32[4,32,256]{2,1,0:T(8,128)} %get-tuple-element.18), channel_id=1, source_target_pairs={{0,16},{16,32},{32,48},{48,64},{64,80},{80,96},{96,112},{112,128},... | collective-permute-start | bytes 393224 | tf_op jit(solution)/shard_map/ppermute | solution.py:427
  6.8 12.3 %collective-permute-start.1 = (f32[4,32,256]{2,1,0:T(8,128)}, f32[4,32,256]{2,1,0:T(8,128)S(1)}, u32[]{:S(2)}, u32[]{:S(2)}) collective-permute-start(f32[4,32,256]{2,1,0:T(8,128)} %get-tuple-element.19), channel_id=1, source_target_pairs={{0,496},{16,0},{32,16},{48,32},{64,48},{80,64},{96,80},{112,96},{1... | collective-permute-start | bytes 393224 | tf_op jit(solution)/shard_map/ppermute | solution.py:427
  19.1 3.9 %collective-permute-start.2 = (f32[4,16,256]{2,1,0:T(8,128)}, f32[4,16,256]{2,1,0:T(8,128)S(1)}, u32[]{:S(2)}, u32[]{:S(2)}) collective-permute-start(f32[4,16,256]{2,1,0:T(8,128)} %get-tuple-element.20), channel_id=1, source_target_pairs={{0,1},{1,2},{2,3},{3,4},{4,5},{5,6},{6,7},{7,8},{8,9},{9,10},{10,1... | collective-permute-start | bytes 196616 | tf_op jit(solution)/shard_map/ppermute | solution.py:427
  23.1 1.9 %collective-permute-start.3 = (f32[4,16,256]{2,1,0:T(8,128)}, f32[4,16,256]{2,1,0:T(8,128)S(1)}, u32[]{:S(2)}, u32[]{:S(2)}) collective-permute-start(f32[4,16,256]{2,1,0:T(8,128)} %get-tuple-element.21), channel_id=1, source_target_pairs={{0,15},{1,0},{2,1},{3,2},{4,3},{5,4},{6,5},{7,6},{8,7},{9,8},{10,9... | collective-permute-start | bytes 196616 | tf_op jit(solution)/shard_map/ppermute | solution.py:427
  25.0 0.0 collective-permute-done.2.ylo
  25.0 0.0 copy-start.4
  25.0 3.8 %collective-permute-done.3.yhi = f32[4,16,256]{2,1,0:T(8,128)S(1)} collective-permute-done((f32[4,16,256]{2,1,0:T(8,128)}, f32[4,16,256]{2,1,0:T(8,128)S(1)}, u32[]{:S(2)}, u32[]{:S(2)}) %collective-permute-start.3) | collective-permute-done | bytes 65568 | tf_op jit(solution)/shard_map/ppermute | solution.py:427
  28.8 0.0 copy-start.5
  28.9 0.0 collective-permute-done.xlo
  28.9 0.0 copy-start.2
  28.9 0.0 collective-permute-done.1.xhi
  28.9 0.0 copy-done.4
  28.9 0.6 copy-done.5
  29.5 0.0 copy-done.2
  29.5 0.0 copy-start.3
  29.5 0.7 copy-done.3
  30.2 8.3 %predict.1 = (f32[16,32,256]{2,1,0:T(8,128)}, f32[16,32,256]{2,1,0:T(8,128)}, f32[16,32,256]{2,1,0:T(8,128)}, f32[16,32,256]{2,1,0:T(8,128)}, f32[16,72,128]{2,1,0:T(8,128)}) custom-call(f32[16,32,256]{2,1,0:T(8,128)} %fd.1, f32[16,32,256]{2,1,0:T(8,128)} %fc.1, f32[16,32,256]{2,1,0:T(8,128)} %fu.1, f32[16,32,256]{2,1,0:T(8,128)} %ft.1, ...), custom_call_target="tpu_custom_call" | custom-call | tf_op jit(solution)/shard_map/predict/pallas_call | solution.py:191
  38.5 0.0 copy-start.7
  38.5 6.2 %all-to-all-start = ((f32[16,72,128]{2,1,0:T(8,128)}), f32[16,72,128]{2,1,0:T(8,128)S(1)}, u32[]{:S(2)}, u32[]{:S(2)}) async-start(f32[16,72,128]{2,1,0:T(8,128)} %get-tuple-element.22), calls=%async_computation | async-start | bytes 1179648 | tf_op jit(solution)/shard_map/all_to_all | solution.py:454
  44.7 0.0 copy-start.6
  44.7 0.0 copy-done.7
  44.7 0.1 dynamic_slice.6
  44.8 0.6 copy-done.6
  45.3 0.7 broadcast_add_fusion.mu
  46.0 9.2 %all-to-all-done.recv = f32[16,72,128]{2,1,0:T(8,128)S(1)} async-done(((f32[16,72,128]{2,1,0:T(8,128)}), f32[16,72,128]{2,1,0:T(8,128)S(1)}, u32[]{:S(2)}, u32[]{:S(2)}) %all-to-all-start) | async-done | bytes 589856 | tf_op jit(solution)/shard_map/all_to_all | solution.py:454
  55.2 0.0 copy-start
  55.2 0.8 copy-done
  56.0 3.2 %transform.1 = (f32[272,512]{1,0:T(8,128)}, f32[32,4,128]{2,1,0:T(4,128)}) custom-call(f32[16,72,128]{2,1,0:T(8,128)} %copy-done, f32[16,512]{1,0:T(8,128)} %broadcast_add_fusion.mu, bf16[384,512]{1,0:T(8,128)(2,1)} %constant.66.clone.high, bf16[384,512]{1,0:T(8,128)(2,1)} %constant.67.clone.low), custom_call_target="tpu_custom_call" | custom-call | tf_op jit(solution)/shard_map/transform/pallas_call | solution.py:263
  59.3 7.0 %all-to-all-start.1 = ((f32[32,4,128]{2,1,0:T(4,128)}), f32[32,4,128]{2,1,0:T(4,128)S(1)}, u32[]{:S(2)}, u32[]{:S(2)}) async-start(f32[32,4,128]{2,1,0:T(4,128)} %get-tuple-element.24), calls=%async_computation.1 | async-start | bytes 131072 | tf_op jit(solution)/shard_map/all_to_all | solution.py:455
  66.3 1.3 %dynamic_slice.7.mu = f32[4,128]{1,0:T(4,128)} dynamic-slice(f32[16,512]{1,0:T(8,128)} %broadcast_add_fusion.mu, s32[]{:T(128)S(6)} %select_n.31, s32[]{:T(128)S(6)} %select_n.33), dynamic_slice_sizes={4,128} | dynamic-slice | bytes 4100 | tf_op jit(solution)/shard_map/dynamic_slice | solution.py:448
  67.6 10.0 %all-to-all-done.1.sums = f32[32,4,128]{2,1,0:T(4,128)S(1)} async-done(((f32[32,4,128]{2,1,0:T(4,128)}), f32[32,4,128]{2,1,0:T(4,128)S(1)}, u32[]{:S(2)}, u32[]{:S(2)}) %all-to-all-start.1) | async-done | bytes 65568 | tf_op jit(solution)/shard_map/all_to_all | solution.py:455
  77.6 0.0 copy-start.1
  77.6 0.6 copy-done.1
  78.2 1.6 %carry.1 = f32[32,4,128]{2,1,0:T(4,128)} custom-call(s32[1]{0:T(128)} %bitcast.kind, f32[32,4,128]{2,1,0:T(4,128)} %copy-done.1, f32[4,128]{1,0:T(4,128)} %dynamic_slice.7.mu), custom_call_target="tpu_custom_call" | custom-call | tf_op jit(solution)/shard_map/carry/pallas_call | solution.py:304
  79.9 15.8 %all_to_all.20.carries = f32[32,4,128]{2,1,0:T(4,128)} all-to-all(f32[32,4,128]{2,1,0:T(4,128)} %carry.1), channel_id=1, replica_groups=mesh['aisle'=32,'span'=16] {'aisle'}, dimensions={0} | all-to-all | bytes 131072 | tf_op jit(solution)/shard_map/all_to_all | solution.py:456
  95.6 3.3 %inverse.1 = f32[16,72,128]{2,1,0:T(8,128)} custom-call(f32[272,512]{1,0:T(8,128)} %get-tuple-element.23.local, f32[32,4,128]{2,1,0:T(4,128)} %all_to_all.20.carries, f32[16,512]{1,0:T(8,128)} %broadcast_add_fusion.mu, f32[1,512]{1,0:T(1,128)} %constant.73.weight, bf16[384,512]{1,0:T(8,128)(2,1)} %constant.66.clone.high, bf16[384,512]{1,0:T(8,128)(2,1)} %constant.67.clone.low), custom_call_target="tpu_custom_call" | custom-call | tf_op jit(solution)/shard_map/inverse/pallas_call | solution.py:369
  98.9 19.1 %all_to_all.21.recv = f32[16,72,128]{2,1,0:T(8,128)} all-to-all(f32[16,72,128]{2,1,0:T(8,128)} %inverse.1), channel_id=1, replica_groups=mesh['aisle'=32,'span'=16] {'span'}, dimensions={0} | all-to-all | bytes 1179648 | tf_op jit(solution)/shard_map/all_to_all | solution.py:457
  118.0 4.7 %correct.1 = (f32[16,32,256]{2,1,0:T(8,128)}, f32[16,32,256]{2,1,0:T(8,128)}, f32[16,32,256]{2,1,0:T(8,128)}) custom-call(f32[16,72,128]{2,1,0:T(8,128)} %all_to_all.21.recv, f32[256,256]{1,0:T(8,128)} %basis.3, f32[16,32,256]{2,1,0:T(8,128)} %get-tuple-element.25.es, f32[16,32,256]{2,1,0:T(8,128)} %get-tuple-element.26.ns, f32[16,32,256]{2,1,0:T(8,128)} %get-tuple-element.27.us), custom_call_target="tpu_custom_call" | custom-call | tf_op jit(solution)/shard_map/correct/pallas_call | solution.py:416
Async XLA Ops:
  2.8 26.1 %collective-permute-start = (f32[4,32,256]{2,1,0:T(8,128)}, f32[4,32,256]{2,1,0:T(8,128)S(1)}, u32[]{:S(2)}, u32[]{:S(2)}) collective-permute-start(f32[4,32,256]{2,1,0:T(8,128)} %get-tuple-element.18), channel_id=1, source_target_pairs={{0,16},{16,32},{32,48},{48,64},{64,80},{80,96},{96,112},{112,128},... | collective-permute-start | bytes 393224 | tf_op jit(solution)/shard_map/ppermute | solution.py:427
  6.8 22.0 %collective-permute-start.1 = (f32[4,32,256]{2,1,0:T(8,128)}, f32[4,32,256]{2,1,0:T(8,128)S(1)}, u32[]{:S(2)}, u32[]{:S(2)}) collective-permute-start(f32[4,32,256]{2,1,0:T(8,128)} %get-tuple-element.19), channel_id=1, source_target_pairs={{0,496},{16,0},{32,16},{48,32},{64,48},{80,64},{96,80},{112,96},{1... | collective-permute-start | bytes 393224 | tf_op jit(solution)/shard_map/ppermute | solution.py:427
  19.1 5.9 %collective-permute-start.2 = (f32[4,16,256]{2,1,0:T(8,128)}, f32[4,16,256]{2,1,0:T(8,128)S(1)}, u32[]{:S(2)}, u32[]{:S(2)}) collective-permute-start(f32[4,16,256]{2,1,0:T(8,128)} %get-tuple-element.20), channel_id=1, source_target_pairs={{0,1},{1,2},{2,3},{3,4},{4,5},{5,6},{6,7},{7,8},{8,9},{9,10},{10,1... | collective-permute-start | bytes 196616 | tf_op jit(solution)/shard_map/ppermute | solution.py:427
  23.1 5.8 %collective-permute-start.3 = (f32[4,16,256]{2,1,0:T(8,128)}, f32[4,16,256]{2,1,0:T(8,128)S(1)}, u32[]{:S(2)}, u32[]{:S(2)}) collective-permute-start(f32[4,16,256]{2,1,0:T(8,128)} %get-tuple-element.21), channel_id=1, source_target_pairs={{0,15},{1,0},{2,1},{3,2},{4,3},{5,4},{6,5},{7,6},{8,7},{9,8},{10,9... | collective-permute-start | bytes 196616 | tf_op jit(solution)/shard_map/ppermute | solution.py:427
  25.0 3.9 %copy-start.4 = (f32[4,16,256]{2,1,0:T(8,128)}, f32[4,16,256]{2,1,0:T(8,128)S(1)}, u32[]{:S(2)}) copy-start(f32[4,16,256]{2,1,0:T(8,128)S(1)} %collective-permute-done.2.ylo) | copy-start | bytes 196612
  28.8 0.6 copy-start.5
  28.9 0.7 copy-start.2
  29.5 0.7 copy-start.3
  38.5 6.2 %copy-start.7 = (f32[256]{0:T(256)S(1)}, f32[256]{0:T(256)}, u32[]{:S(2)}) copy-start(f32[256]{0:T(256)} %param.17) | copy-start | bytes 3076
  38.5 16.7 %all-to-all-start = ((f32[16,72,128]{2,1,0:T(8,128)}), f32[16,72,128]{2,1,0:T(8,128)S(1)}, u32[]{:S(2)}, u32[]{:S(2)}) async-start(f32[16,72,128]{2,1,0:T(8,128)} %get-tuple-element.22), calls=%async_computation | async-start | bytes 1179648 | tf_op jit(solution)/shard_map/all_to_all | solution.py:454
  44.7 0.7 copy-start.6
  55.2 0.8 copy-start
  59.3 18.3 %all-to-all-start.1 = ((f32[32,4,128]{2,1,0:T(4,128)}), f32[32,4,128]{2,1,0:T(4,128)S(1)}, u32[]{:S(2)}, u32[]{:S(2)}) async-start(f32[32,4,128]{2,1,0:T(4,128)} %get-tuple-element.24), calls=%async_computation.1 | async-start | bytes 131072 | tf_op jit(solution)/shard_map/all_to_all | solution.py:455
  77.6 0.6 copy-start.1
where the time goes:
time: 124 us; the launch traced here: 123 us
  starting transfers between devices  35.3 us (28%)
  blocking collectives  34.9 us (28%)
  Pallas kernels  23.3 us (19%)
  waiting for transfers between devices  23 us (19%)
  local copies, waits for them, and re-layouts  4.76 us (4%)
    ppermute x4, starting transfers between devices, ring(): lax.ppermute(value, axis, [(i, (i + step) % count) for i in range(count)])  22.2 us
    all_to_all x1, blocking collectives, per_device(): swap(chunk, 'span')  19.1 us
    all_to_all x1, blocking collectives, per_device(): chunk = inverse(local, swap(carries, 'aisle'), mu, weight, high, low)  15.8 us
    all_to_all x1, waiting for transfers between devices, per_device(): carries = carry(kind, swap(sums, 'aisle'), mu_lines)  9.96 us
    all_to_all x1, waiting for transfers between devices, per_device(): local, sums = transform(swap(chunk, 'span'), mu, high, low)  9.17 us
    pallas_call x1, Pallas kernels, predict(): pl.pallas_call(predict_kernel, in_specs=[any_spec] * 6 + [vmem] * 3, out_...  8.27 us
    all_to_all x1, starting transfers between devices, per_device(): carries = carry(kind, swap(sums, 'aisle'), mu_lines)  6.97 us
    all_to_all x1, starting transfers between devices, per_device(): local, sums = transform(swap(chunk, 'span'), mu, high, low)  6.18 us
  transfers between devices with their start and end apart: 6, of which 3 were waited for; matrix products, arithmetic and copies ran while one was open for 2% of the time, Pallas kernels for 0%

commit v1 on v0

--- a/solution.py
+++ b/solution.py
@@ -91,6 +91,10 @@
     return vectors
 
 
+def near(value):
+    return pltpu.with_memory_space_constraint(value, pltpu.VMEM)
+
+
 def pack_kernel(*refs):
     x_first, x_last, y_first, y_last = refs[16:]
     for f in range(4):
@@ -116,19 +120,27 @@
 
 
 def predict_kernel(
-    fd, fc, fu, ft, xlo, xhi, ylo, yhi, basis, es, ns, us, ts, chunk, buf, src, sems
+    fd, fc, fu, ft, xlo, xhi, ylo, yhi, basis, es, ns, us, ts, chunk, buf, src, out, sems, done
 ):
-    copies = [pltpu.make_async_copy(f, buf.at[i, pl.ds(1, BX)], sems.at[i]) for i, f in enumerate((fd, fc, fu, ft))]
-    copies.append(pltpu.make_async_copy(xlo, buf.at[:, 0], sems.at[4]))
-    copies.append(pltpu.make_async_copy(xhi, buf.at[:, BX + 1], sems.at[5]))
-    for copy in copies:
-        copy.start()
+    loads = []
+    for t in range(4):
+        first, last = (4 * t + 1 if t else 0), min(4 * t + 5, BX)
+        loads.append(
+            [
+                pltpu.make_async_copy(
+                    f.at[pl.ds(first, last - first)], buf.at[i, pl.ds(first + 1, last - first)], sems.at[t, i]
+                )
+                for i, f in enumerate((fd, fc, fu, ft))
+            ]
+        )
+        for copy in loads[t]:
+            copy.start()
+    buf[:, 0] = xlo[...]
+    buf[:, BX + 1] = xhi[...]
     row = lax.broadcasted_iota(jnp.int32, (BY, NZ), 0)
     lane = lax.broadcasted_iota(jnp.int32, (BY, NZ), 1)
     base = BX * BY
     src[base + BY :, :] = jnp.zeros((128 - BY, NZ), f32)
-    for copy in copies:
-        copy.wait()
     zero = jnp.zeros((BY, NZ), f32)
 
     def south_of(value, edge):
@@ -161,16 +173,23 @@
                 tendency = tendency + buoyancy * centre[3]
             stars.append(centre[f] + step_gain * tendency)
         east, north, upward, heat = stars
-        es[x] = east
-        ns[x] = north
-        us[x] = upward
-        ts[x] = heat
+        for f in range(4):
+            out[f, x] = stars[f]
         flux = (east - east_prev) + (north - south_of(north, zero)) + (upward - lower_of(upward))
         src[pl.ds(pl.multiple_of(x * BY, BY), BY), :] = flux
         src[pl.ds(base + BY + x, 1), :] = -north[BY - 1 :, :]
         return east
 
-    last = lax.fori_loop(0, BX, plane, zero)
+    last = zero
+    stores = []
+    for t in range(4):
+        for copy in loads[t]:
+            copy.wait()
+        last = lax.fori_loop(4 * t, 4 * t + 4, plane, last)
+        for f, ref in enumerate((es, ns, us, ts)):
+            copy = pltpu.make_async_copy(out.at[f, pl.ds(4 * t, 4)], ref.at[pl.ds(4 * t, 4)], done.at[t, f])
+            copy.start()
+            stores.append(copy)
     src[base : base + BY, :] = -last
     forward = split(basis[...])
     for t in range(5):
@@ -182,6 +201,8 @@
             lanes = lax.broadcasted_iota(jnp.int32, (8, 128), 1)
             for s in range(SPAN):
                 chunk[s, 4 * KS :, :] = jnp.where(lanes < 64, modes[s, 0], pltpu.roll(modes[s, 1], 64, 1))
+    for copy in stores:
+        copy.wait()
 
 
 def predict(fields, xlo, xhi, ylo, yhi, basis):
@@ -190,16 +211,18 @@
     block = jax.ShapeDtypeStruct((BX, BY, NZ), f32)
     return pl.pallas_call(
         predict_kernel,
-        in_specs=[any_spec] * 6 + [vmem] * 3,
-        out_specs=[vmem] * 5,
+        in_specs=[any_spec] * 4 + [vmem] * 5,
+        out_specs=[any_spec] * 4 + [vmem],
         out_shape=[block] * 4 + [jax.ShapeDtypeStruct((SPAN, ROWS, 128), f32)],
         scratch_shapes=[
             pltpu.VMEM((4, BX + 2, BY, NZ), f32),
             pltpu.VMEM((BX * BY + 128, NZ), f32),
-            pltpu.SemaphoreType.DMA((6,)),
+            pltpu.VMEM((4, BX, BY, NZ), f32),
+            pltpu.SemaphoreType.DMA((4, 4)),
+            pltpu.SemaphoreType.DMA((4, 4)),
         ],
         name="predict",
-    )(*fields, xlo, xhi, ylo, yhi, basis)
+    )(*fields, near(xlo), near(xhi), near(ylo), near(yhi), basis)
 
 
 def decay(mu):
@@ -270,7 +293,7 @@
         ],
         scratch_shapes=[pltpu.VMEM((XR * KS, NY), f32), pltpu.VMEM((XR * KS, 128), f32)],
         name="transform",
-    )(recv, mu, high, low)
+    )(near(recv), mu, high, low)
 
 
 def carry_kernel(kind, sums, mu, carries):
@@ -307,7 +330,7 @@
         out_specs=vmem,
         out_shape=jax.ShapeDtypeStruct((AISLE, 4, 128), f32),
         name="carry",
-    )(kind, sums, mu)
+    )(kind, near(sums), mu)
 
 
 def inverse_kernel(local, carries, mu, weight, high, low, chunk, ends, work_high, work_low, work, extra):
@@ -379,10 +402,13 @@
             pltpu.VMEM((XR * KS, 128), f32),
         ],
         name="inverse",
-    )(local, carries, mu, weight, high, low)
-
-
-def correct_kernel(recv, basis, es, ns, us, east, north, upward, press):
+    )(local, near(carries), mu, weight, high, low)
+
+
+def correct_kernel(recv, basis, es, ns, us, east, north, upward, press, buf, sems, done):
+    loads = [pltpu.make_async_copy(ref, buf.at[f], sems.at[f]) for f, ref in enumerate((es, ns, us))]
+    for copy in loads:
+        copy.start()
     back = split(basis[...])
     for t in range(4):
         modes = split(recv[:, t * KS : (t + 1) * KS, :].reshape(NZ, 128))
@@ -402,25 +428,41 @@
         edge = press[pl.ds(BX * BY + BY + x, 1), :]
         beside = jnp.where(row == BY - 1, edge, pltpu.roll(here, BY - 1, 0))
         above = jnp.where(lane == NZ - 1, 0.0, pltpu.roll(here, NZ - 1, 1))
-        east[x] = es[x] - (beyond - here)
-        north[x] = ns[x] - (beside - here)
-        upward[x] = us[x] - (above - here)
+        for f, value in enumerate((beyond, beside, above)):
+            buf[f, x] = buf[f, x] - (value - here)
         return beyond
 
-    lax.fori_loop(0, BX, plane, press[:BY, :])
+    for copy in loads:
+        copy.wait()
+    here = press[:BY, :]
+    stores = []
+    for t in range(4):
+        here = lax.fori_loop(4 * t, 4 * t + 4, plane, here)
+        for f, ref in enumerate((east, north, upward)):
+            copy = pltpu.make_async_copy(buf.at[f, pl.ds(4 * t, 4)], ref.at[pl.ds(4 * t, 4)], done.at[t, f])
+            copy.start()
+            stores.append(copy)
+    for copy in stores:
+        copy.wait()
 
 
 def correct(recv, basis, es, ns, us):
+    any_spec = pl.BlockSpec(memory_space=pl.ANY)
     vmem = pl.BlockSpec(memory_space=pltpu.VMEM)
     block = jax.ShapeDtypeStruct((BX, BY, NZ), f32)
     return pl.pallas_call(
         correct_kernel,
-        in_specs=[vmem] * 5,
-        out_specs=[vmem] * 3,
+        in_specs=[vmem] * 2 + [any_spec] * 3,
+        out_specs=[any_spec] * 3,
         out_shape=[block] * 3,
-        scratch_shapes=[pltpu.VMEM((BX * BY + 128, NZ), f32)],
+        scratch_shapes=[
+            pltpu.VMEM((BX * BY + 128, NZ), f32),
+            pltpu.VMEM((3, BX, BY, NZ), f32),
+            pltpu.SemaphoreType.DMA((3,)),
+            pltpu.SemaphoreType.DMA((4, 3)),
+        ],
         name="correct",
-    )(recv, basis, es, ns, us)
+    )(near(recv), basis, es, ns, us)
 
 
 def ring(axis, count, step, value):

time: 124 us -> 119 us (0.960)
  local copies, waits for them, and re-layouts: 4.76 us -> 2.01 us
  blocking collectives: 34.9 us -> 33.5 us
    unnamed x16 -> x4, local copies, waits for them, and re-layouts: 3.35 us -> 0.59 us
where the time goes in v1:
time: 119 us; the launch traced here: 118 us
  starting transfers between devices  35.3 us (30%)
  blocking collectives  33.5 us (28%)
  waiting for transfers between devices  23 us (19%)
  Pallas kernels  22.7 us (19%)
  local copies, waits for them, and re-layouts  2.01 us (2%)
    ppermute x4, starting transfers between devices, ring(): lax.ppermute(value, axis, [(i, (i + step) % count) for i in range(count)])  22.2 us
    all_to_all x1, blocking collectives, per_device(): swap(chunk, 'span')  18.4 us
    all_to_all x1, blocking collectives, per_device(): chunk = inverse(local, swap(carries, 'aisle'), mu, weight, high, low)  15.1 us
    all_to_all x1, waiting for transfers between devices, per_device(): carries = carry(kind, swap(sums, 'aisle'), mu_lines)  9.95 us
    all_to_all x1, waiting for transfers between devices, per_device(): local, sums = transform(swap(chunk, 'span'), mu, high, low)  9.17 us
    pallas_call x1, Pallas kernels, predict(): pl.pallas_call(predict_kernel, in_specs=[any_spec] * 4 + [vmem] * 5, out_...  7.92 us
    all_to_all x1, starting transfers between devices, per_device(): carries = carry(kind, swap(sums, 'aisle'), mu_lines)  6.97 us
    all_to_all x1, starting transfers between devices, per_device(): local, sums = transform(swap(chunk, 'span'), mu, high, low)  6.19 us
  transfers between devices with their start and end apart: 6, of which 3 were waited for; matrix products, arithmetic and copies ran while one was open for 2% of the time, Pallas kernels for 0%

profile of v1, /device:TPU:1, one launch (start us, length us, event | category | flops | bytes accessed | tf_op | source)
XLA Modules:
  0.0 118.0 jit_solution(7567425177393045726)
XLA Ops:
  0.6 2.2 %pack.1 = (f32[4,32,256]{2,1,0:T(8,128)}, f32[4,32,256]{2,1,0:T(8,128)}, f32[4,16,256]{2,1,0:T(8,128)}, f32[4,16,256]{2,1,0:T(8,128)}) custom-call(f32[16,32,256]{2,1,0:T(8,128)} %fd.1, f32[16,32,256]{2,1,0:T(8,128)} %fc.1, f32[16,32,256]{2,1,0:T(8,128)} %fu.1, f32[16,32,256]{2,1,0:T(8,128)} %ft.1, f32[16,32,256]{2,1,0:T(8,128)} %fd.1, f32[16,32,256]{2,1,0:T(8,128)} %fc.1, ...), custom_call_target="tpu_custom_call" | custom-call | tf_op jit(solution)/shard_map/pack/pallas_call | solution.py:112
  2.8 4.0 %collective-permute-start = (f32[4,32,256]{2,1,0:T(8,128)}, f32[4,32,256]{2,1,0:T(8,128)S(1)}, u32[]{:S(2)}, u32[]{:S(2)}) collective-permute-start(f32[4,32,256]{2,1,0:T(8,128)} %get-tuple-element.18), channel_id=1, source_target_pairs={{0,16},{16,32},{32,48},{48,64},{64,80},{80,96},{96,112},{112,128},... | collective-permute-start | bytes 393224 | tf_op jit(solution)/shard_map/ppermute | solution.py:469
  6.8 12.3 %collective-permute-start.1 = (f32[4,32,256]{2,1,0:T(8,128)}, f32[4,32,256]{2,1,0:T(8,128)S(1)}, u32[]{:S(2)}, u32[]{:S(2)}) collective-permute-start(f32[4,32,256]{2,1,0:T(8,128)} %get-tuple-element.19), channel_id=1, source_target_pairs={{0,496},{16,0},{32,16},{48,32},{64,48},{80,64},{96,80},{112,96},{1... | collective-permute-start | bytes 393224 | tf_op jit(solution)/shard_map/ppermute | solution.py:469
  19.1 3.9 %collective-permute-start.2 = (f32[4,16,256]{2,1,0:T(8,128)}, f32[4,16,256]{2,1,0:T(8,128)S(1)}, u32[]{:S(2)}, u32[]{:S(2)}) collective-permute-start(f32[4,16,256]{2,1,0:T(8,128)} %get-tuple-element.20), channel_id=1, source_target_pairs={{0,1},{1,2},{2,3},{3,4},{4,5},{5,6},{6,7},{7,8},{8,9},{9,10},{10,1... | collective-permute-start | bytes 196616 | tf_op jit(solution)/shard_map/ppermute | solution.py:469
  23.1 1.9 %collective-permute-start.3 = (f32[4,16,256]{2,1,0:T(8,128)}, f32[4,16,256]{2,1,0:T(8,128)S(1)}, u32[]{:S(2)}, u32[]{:S(2)}) collective-permute-start(f32[4,16,256]{2,1,0:T(8,128)} %get-tuple-element.21), channel_id=1, source_target_pairs={{0,15},{1,0},{2,1},{3,2},{4,3},{5,4},{6,5},{7,6},{8,7},{9,8},{10,9... | collective-permute-start | bytes 196616 | tf_op jit(solution)/shard_map/ppermute | solution.py:469
  25.0 0.0 collective-permute-done.2.ylo
  25.0 3.9 %collective-permute-done.3.yhi = f32[4,16,256]{2,1,0:T(8,128)S(1)} collective-permute-done((f32[4,16,256]{2,1,0:T(8,128)}, f32[4,16,256]{2,1,0:T(8,128)S(1)}, u32[]{:S(2)}, u32[]{:S(2)}) %collective-permute-start.3) | collective-permute-done | bytes 65568 | tf_op jit(solution)/shard_map/ppermute | solution.py:469
  28.8 0.0 collective-permute-done.xlo
  28.9 0.0 collective-permute-done.1.xhi
  28.9 7.9 %predict.1 = (f32[16,32,256]{2,1,0:T(8,128)}, f32[16,32,256]{2,1,0:T(8,128)}, f32[16,32,256]{2,1,0:T(8,128)}, f32[16,32,256]{2,1,0:T(8,128)}, f32[16,72,128]{2,1,0:T(8,128)}) custom-call(f32[16,32,256]{2,1,0:T(8,128)} %fd.1, f32[16,32,256]{2,1,0:T(8,128)} %fc.1, f32[16,32,256]{2,1,0:T(8,128)} %fu.1, f32[16,32,256]{2,1,0:T(8,128)} %ft.1, ...), custom_call_target="tpu_custom_call" | custom-call | tf_op jit(solution)/shard_map/predict/pallas_call | solution.py:212
  36.8 0.0 copy-start.1
  36.8 6.2 %all-to-all-start = ((f32[16,72,128]{2,1,0:T(8,128)}), f32[16,72,128]{2,1,0:T(8,128)S(1)}, u32[]{:S(2)}, u32[]{:S(2)}) async-start(f32[16,72,128]{2,1,0:T(8,128)} %get-tuple-element.22), calls=%async_computation | async-start | bytes 1179648 | tf_op jit(solution)/shard_map/all_to_all | solution.py:496
  43.0 0.0 copy-start
  43.0 0.0 copy-done.1
  43.0 0.1 dynamic_slice.6
  43.1 0.6 copy-done
  43.7 0.7 broadcast_add_fusion.mu
  44.3 9.2 %all-to-all-done.recv = f32[16,72,128]{2,1,0:T(8,128)S(1)} async-done(((f32[16,72,128]{2,1,0:T(8,128)}), f32[16,72,128]{2,1,0:T(8,128)S(1)}, u32[]{:S(2)}, u32[]{:S(2)}) %all-to-all-start) | async-done | bytes 589856 | tf_op jit(solution)/shard_map/all_to_all | solution.py:496
  53.5 3.0 %transform.1 = (f32[272,512]{1,0:T(8,128)}, f32[32,4,128]{2,1,0:T(4,128)}) custom-call(f32[16,72,128]{2,1,0:T(8,128)S(1)} %all-to-all-done.recv, f32[16,512]{1,0:T(8,128)} %broadcast_add_fusion.mu, bf16[384,512]{1,0:T(8,128)(2,1)} %constant.66.clone.high, bf16[384,512]{1,0:T(8,128)(2,1)} %constant.67.clone.low), custom_call_target="tpu_custom_call" | custom-call | tf_op jit(solution)/shard_map/transform/pallas_call | solution.py:286
  56.6 7.0 %all-to-all-start.1 = ((f32[32,4,128]{2,1,0:T(4,128)}), f32[32,4,128]{2,1,0:T(4,128)S(1)}, u32[]{:S(2)}, u32[]{:S(2)}) async-start(f32[32,4,128]{2,1,0:T(4,128)} %get-tuple-element.24), calls=%async_computation.1 | async-start | bytes 131072 | tf_op jit(solution)/shard_map/all_to_all | solution.py:497
  63.6 1.3 %dynamic_slice.7.mu = f32[4,128]{1,0:T(4,128)} dynamic-slice(f32[16,512]{1,0:T(8,128)} %broadcast_add_fusion.mu, s32[]{:T(128)S(6)} %select_n.31, s32[]{:T(128)S(6)} %select_n.33), dynamic_slice_sizes={4,128} | dynamic-slice | bytes 4100 | tf_op jit(solution)/shard_map/dynamic_slice | solution.py:490
  64.9 10.0 %all-to-all-done.1.sums = f32[32,4,128]{2,1,0:T(4,128)S(1)} async-done(((f32[32,4,128]{2,1,0:T(4,128)}), f32[32,4,128]{2,1,0:T(4,128)S(1)}, u32[]{:S(2)}, u32[]{:S(2)}) %all-to-all-start.1) | async-done | bytes 65568 | tf_op jit(solution)/shard_map/all_to_all | solution.py:497
  74.9 1.5 %carry.1 = f32[32,4,128]{2,1,0:T(4,128)} custom-call(s32[1]{0:T(128)} %bitcast.kind, f32[32,4,128]{2,1,0:T(4,128)S(1)} %all-to-all-done.1.sums, f32[4,128]{1,0:T(4,128)} %dynamic_slice.7.mu), custom_call_target="tpu_custom_call" | custom-call | tf_op jit(solution)/shard_map/carry/pallas_call | solution.py:327
  76.4 15.1 %all_to_all.20.carries = f32[32,4,128]{2,1,0:T(4,128)S(1)} all-to-all(f32[32,4,128]{2,1,0:T(4,128)} %carry.1), channel_id=1, replica_groups=mesh['aisle'=32,'span'=16] {'aisle'}, dimensions={0} | all-to-all | bytes 131072 | tf_op jit(solution)/shard_map/all_to_all | solution.py:498
  91.5 3.2 %inverse.1 = f32[16,72,128]{2,1,0:T(8,128)} custom-call(f32[272,512]{1,0:T(8,128)} %get-tuple-element.23.local, f32[32,4,128]{2,1,0:T(4,128)S(1)} %all_to_all.20.carries, f32[16,512]{1,0:T(8,128)} %broadcast_add_fusion.mu, f32[1,512]{1,0:T(1,128)} %constant.73.weight, bf16[384,512]{1,0:T(8,128)(2,1)} %constant.66.clone.high, bf16[384,512]{1,0:T(8,128)(2,1)} %constant.67.clone.low), custom_call_target="tpu_custom_call" | custom-call | tf_op jit(solution)/shard_map/inverse/pallas_call | solution.py:392
  94.7 18.4 %all_to_all.21.recv = f32[16,72,128]{2,1,0:T(8,128)S(1)} all-to-all(f32[16,72,128]{2,1,0:T(8,128)} %inverse.1), channel_id=1, replica_groups=mesh['aisle'=32,'span'=16] {'span'}, dimensions={0} | all-to-all | bytes 1179648 | tf_op jit(solution)/shard_map/all_to_all | solution.py:499
  113.1 4.8 %correct.1 = (f32[16,32,256]{2,1,0:T(8,128)}, f32[16,32,256]{2,1,0:T(8,128)}, f32[16,32,256]{2,1,0:T(8,128)}) custom-call(f32[16,72,128]{2,1,0:T(8,128)S(1)} %all_to_all.21.recv, f32[256,256]{1,0:T(8,128)} %basis.3, f32[16,32,256]{2,1,0:T(8,128)} %get-tuple-element.25.es, f32[16,32,256]{2,1,0:T(8,128)} %get-tuple-element.26.ns, ...), custom_call_target="tpu_custom_call" | custom-call | tf_op jit(solution)/shard_map/correct/pallas_call | solution.py:453
Async XLA Ops:
  2.8 26.1 %collective-permute-start = (f32[4,32,256]{2,1,0:T(8,128)}, f32[4,32,256]{2,1,0:T(8,128)S(1)}, u32[]{:S(2)}, u32[]{:S(2)}) collective-permute-start(f32[4,32,256]{2,1,0:T(8,128)} %get-tuple-element.18), channel_id=1, source_target_pairs={{0,16},{16,32},{32,48},{48,64},{64,80},{80,96},{96,112},{112,128},... | collective-permute-start | bytes 393224 | tf_op jit(solution)/shard_map/ppermute | solution.py:469
  6.8 22.0 %collective-permute-start.1 = (f32[4,32,256]{2,1,0:T(8,128)}, f32[4,32,256]{2,1,0:T(8,128)S(1)}, u32[]{:S(2)}, u32[]{:S(2)}) collective-permute-start(f32[4,32,256]{2,1,0:T(8,128)} %get-tuple-element.19), channel_id=1, source_target_pairs={{0,496},{16,0},{32,16},{48,32},{64,48},{80,64},{96,80},{112,96},{1... | collective-permute-start | bytes 393224 | tf_op jit(solution)/shard_map/ppermute | solution.py:469
  19.1 5.9 %collective-permute-start.2 = (f32[4,16,256]{2,1,0:T(8,128)}, f32[4,16,256]{2,1,0:T(8,128)S(1)}, u32[]{:S(2)}, u32[]{:S(2)}) collective-permute-start(f32[4,16,256]{2,1,0:T(8,128)} %get-tuple-element.20), channel_id=1, source_target_pairs={{0,1},{1,2},{2,3},{3,4},{4,5},{5,6},{6,7},{7,8},{8,9},{9,10},{10,1... | collective-permute-start | bytes 196616 | tf_op jit(solution)/shard_map/ppermute | solution.py:469
  23.1 5.8 %collective-permute-start.3 = (f32[4,16,256]{2,1,0:T(8,128)}, f32[4,16,256]{2,1,0:T(8,128)S(1)}, u32[]{:S(2)}, u32[]{:S(2)}) collective-permute-start(f32[4,16,256]{2,1,0:T(8,128)} %get-tuple-element.21), channel_id=1, source_target_pairs={{0,15},{1,0},{2,1},{3,2},{4,3},{5,4},{6,5},{7,6},{8,7},{9,8},{10,9... | collective-permute-start | bytes 196616 | tf_op jit(solution)/shard_map/ppermute | solution.py:469
  36.8 6.2 %copy-start.1 = (f32[256]{0:T(256)S(1)}, f32[256]{0:T(256)}, u32[]{:S(2)}) copy-start(f32[256]{0:T(256)} %param.17) | copy-start | bytes 3076
  36.8 16.7 %all-to-all-start = ((f32[16,72,128]{2,1,0:T(8,128)}), f32[16,72,128]{2,1,0:T(8,128)S(1)}, u32[]{:S(2)}, u32[]{:S(2)}) async-start(f32[16,72,128]{2,1,0:T(8,128)} %get-tuple-element.22), calls=%async_computation | async-start | bytes 1179648 | tf_op jit(solution)/shard_map/all_to_all | solution.py:496
  43.0 0.7 copy-start
  56.6 18.3 %all-to-all-start.1 = ((f32[32,4,128]{2,1,0:T(4,128)}), f32[32,4,128]{2,1,0:T(4,128)S(1)}, u32[]{:S(2)}, u32[]{:S(2)}) async-start(f32[32,4,128]{2,1,0:T(4,128)} %get-tuple-element.24), calls=%async_computation.1 | async-start | bytes 131072 | tf_op jit(solution)/shard_map/all_to_all | solution.py:497

commit v2 on v1

--- a/solution.py
+++ b/solution.py
@@ -222,7 +222,7 @@
             pltpu.SemaphoreType.DMA((4, 4)),
         ],
         name="predict",
-    )(*fields, near(xlo), near(xhi), near(ylo), near(yhi), basis)
+    )(*fields, near(xlo), near(xhi), near(ylo), near(yhi), near(basis))
 
 
 def decay(mu):
@@ -288,12 +288,12 @@
         in_specs=[vmem] * 4,
         out_specs=[vmem] * 2,
         out_shape=[
-            jax.ShapeDtypeStruct((XR * KS, NY), f32),
+            pltpu.VMEM((XR * KS, NY), f32),
             jax.ShapeDtypeStruct((AISLE, 4, 128), f32),
         ],
         scratch_shapes=[pltpu.VMEM((XR * KS, NY), f32), pltpu.VMEM((XR * KS, 128), f32)],
         name="transform",
-    )(near(recv), mu, high, low)
+    )(near(recv), near(mu), near(high), near(low))
 
 
 def carry_kernel(kind, sums, mu, carries):
@@ -330,7 +330,7 @@
         out_specs=vmem,
         out_shape=jax.ShapeDtypeStruct((AISLE, 4, 128), f32),
         name="carry",
-    )(kind, near(sums), mu)
+    )(kind, near(sums), near(mu))
 
 
 def inverse_kernel(local, carries, mu, weight, high, low, chunk, ends, work_high, work_low, work, extra):
@@ -402,7 +402,7 @@
             pltpu.VMEM((XR * KS, 128), f32),
         ],
         name="inverse",
-    )(local, near(carries), mu, weight, high, low)
+    )(near(local), near(carries), near(mu), near(weight), near(high), near(low))
 
 
 def correct_kernel(recv, basis, es, ns, us, east, north, upward, press, buf, sems, done):
@@ -462,7 +462,7 @@
             pltpu.SemaphoreType.DMA((4, 3)),
         ],
         name="correct",
-    )(near(recv), basis, es, ns, us)
+    )(near(recv), near(basis), es, ns, us)
 
 
 def ring(axis, count, step, value):

time: 119 us -> 114 us (0.958)
  Pallas kernels: 22.7 us -> 17.5 us
  waiting for transfers between devices: 23 us -> 24.9 us
  local copies, waits for them, and re-layouts: 2.01 us -> 0.78 us
    pallas_call x1, Pallas kernels: 3.04 us -> 1.71 us  [transform(): pl.pallas_call(transform_kernel, in_specs=[vmem] * 4, out_specs=[vmem] *...]
    pallas_call x1, Pallas kernels: 3.23 us -> 1.92 us  [inverse(): pl.pallas_call(inverse_kernel, in_specs=[vmem] * 6, out_specs=vmem, out_s...]
    all_to_all x1, waiting for transfers between devices: 9.95 us -> 11.2 us  [per_device(): carries = carry(kind, swap(sums, 'aisle'), mu_lines)]
    dynamic_slice x1, local copies, waits for them, and re-layouts: 1.34 us -> 0.08 us  [per_device(): lax.dynamic_slice(mu, (turn // 4 % 4 * 4, turn % 4 * 128), (4, 128))]
  transfers between devices with their start and end apart: 6 -> 6, of which waited for: 3 -> 3; matrix products, arithmetic and copies ran while one was open for 2% -> 0% of each run, Pallas kernels for 0% -> 0%
where the time goes in v2:
time: 114 us; the launch traced here: 113 us
  starting transfers between devices  35.4 us (31%)
  blocking collectives  33.7 us (30%)
  waiting for transfers between devices  24.9 us (22%)
  Pallas kernels  17.5 us (15%)
    ppermute x4, starting transfers between devices, ring(): lax.ppermute(value, axis, [(i, (i + step) % count) for i in range(count)])  22.2 us
    all_to_all x1, blocking collectives, per_device(): swap(chunk, 'span')  18.6 us
    all_to_all x1, blocking collectives, per_device(): chunk = inverse(local, swap(carries, 'aisle'), mu, weight, high, low)  15.1 us
    all_to_all x1, waiting for transfers between devices, per_device(): carries = carry(kind, swap(sums, 'aisle'), mu_lines)  11.2 us
    all_to_all x1, waiting for transfers between devices, per_device(): local, sums = transform(swap(chunk, 'span'), mu, high, low)  9.78 us
    pallas_call x1, Pallas kernels, predict(): pl.pallas_call(predict_kernel, in_specs=[any_spec] * 4 + [vmem] * 5, out_...  6.99 us
    all_to_all x1, starting transfers between devices, per_device(): carries = carry(kind, swap(sums, 'aisle'), mu_lines)  6.96 us
    all_to_all x1, starting transfers between devices, per_device(): local, sums = transform(swap(chunk, 'span'), mu, high, low)  6.32 us
  transfers between devices with their start and end apart: 6, of which 3 were waited for; matrix products, arithmetic and copies ran while one was open for 0% of the time, Pallas kernels for 0%

profile of v2, /device:TPU:1, one launch (start us, length us, event | category | flops | bytes accessed | tf_op | source)
XLA Modules:
  0.0 113.1 jit_solution(3371692585403399626)
XLA Ops:
  0.6 0.0 copy-start.3
  0.6 2.2 %pack.1 = (f32[4,32,256]{2,1,0:T(8,128)}, f32[4,32,256]{2,1,0:T(8,128)}, f32[4,16,256]{2,1,0:T(8,128)}, f32[4,16,256]{2,1,0:T(8,128)}) custom-call(f32[16,32,256]{2,1,0:T(8,128)} %fd.1, f32[16,32,256]{2,1,0:T(8,128)} %fc.1, f32[16,32,256]{2,1,0:T(8,128)} %fu.1, f32[16,32,256]{2,1,0:T(8,128)} %ft.1, f32[16,32,256]{2,1,0:T(8,128)} %fd.1, f32[16,32,256]{2,1,0:T(8,128)} %fc.1, ...), custom_call_target="tpu_custom_call" | custom-call | tf_op jit(solution)/shard_map/pack/pallas_call | solution.py:112
  2.8 4.0 %collective-permute-start = (f32[4,32,256]{2,1,0:T(8,128)}, f32[4,32,256]{2,1,0:T(8,128)S(1)}, u32[]{:S(2)}, u32[]{:S(2)}) collective-permute-start(f32[4,32,256]{2,1,0:T(8,128)} %get-tuple-element.18), channel_id=1, source_target_pairs={{0,16},{16,32},{32,48},{48,64},{64,80},{80,96},{96,112},{112,128},... | collective-permute-start | bytes 393224 | tf_op jit(solution)/shard_map/ppermute | solution.py:469
  6.9 12.3 %collective-permute-start.1 = (f32[4,32,256]{2,1,0:T(8,128)}, f32[4,32,256]{2,1,0:T(8,128)S(1)}, u32[]{:S(2)}, u32[]{:S(2)}) collective-permute-start(f32[4,32,256]{2,1,0:T(8,128)} %get-tuple-element.19), channel_id=1, source_target_pairs={{0,496},{16,0},{32,16},{48,32},{64,48},{80,64},{96,80},{112,96},{1... | collective-permute-start | bytes 393224 | tf_op jit(solution)/shard_map/ppermute | solution.py:469
  19.1 3.9 %collective-permute-start.2 = (f32[4,16,256]{2,1,0:T(8,128)}, f32[4,16,256]{2,1,0:T(8,128)S(1)}, u32[]{:S(2)}, u32[]{:S(2)}) collective-permute-start(f32[4,16,256]{2,1,0:T(8,128)} %get-tuple-element.20), channel_id=1, source_target_pairs={{0,1},{1,2},{2,3},{3,4},{4,5},{5,6},{6,7},{7,8},{8,9},{9,10},{10,1... | collective-permute-start | bytes 196616 | tf_op jit(solution)/shard_map/ppermute | solution.py:469
  23.1 1.9 %collective-permute-start.3 = (f32[4,16,256]{2,1,0:T(8,128)}, f32[4,16,256]{2,1,0:T(8,128)S(1)}, u32[]{:S(2)}, u32[]{:S(2)}) collective-permute-start(f32[4,16,256]{2,1,0:T(8,128)} %get-tuple-element.21), channel_id=1, source_target_pairs={{0,15},{1,0},{2,1},{3,2},{4,3},{5,4},{6,5},{7,6},{8,7},{9,8},{10,9... | collective-permute-start | bytes 196616 | tf_op jit(solution)/shard_map/ppermute | solution.py:469
  25.0 0.0 collective-permute-done.2.ylo
  25.0 3.9 %collective-permute-done.3.yhi = f32[4,16,256]{2,1,0:T(8,128)S(1)} collective-permute-done((f32[4,16,256]{2,1,0:T(8,128)}, f32[4,16,256]{2,1,0:T(8,128)S(1)}, u32[]{:S(2)}, u32[]{:S(2)}) %collective-permute-start.3) | collective-permute-done | bytes 65568 | tf_op jit(solution)/shard_map/ppermute | solution.py:469
  28.9 0.0 collective-permute-done.xlo
  28.9 0.0 collective-permute-done.1.xhi
  28.9 0.0 copy-done.3
  28.9 7.0 %predict.1 = (f32[16,32,256]{2,1,0:T(8,128)}, f32[16,32,256]{2,1,0:T(8,128)}, f32[16,32,256]{2,1,0:T(8,128)}, f32[16,32,256]{2,1,0:T(8,128)}, f32[16,72,128]{2,1,0:T(8,128)}) custom-call(f32[16,32,256]{2,1,0:T(8,128)} %fd.1, f32[16,32,256]{2,1,0:T(8,128)} %fc.1, f32[16,32,256]{2,1,0:T(8,128)} %fu.1, f32[16,32,256]{2,1,0:T(8,128)} %ft.1, ...), custom_call_target="tpu_custom_call" | custom-call | tf_op jit(solution)/shard_map/predict/pallas_call | solution.py:212
  35.9 0.0 copy-start.6
  35.9 0.0 copy-start
  35.9 0.0 copy-start.1
  35.9 6.3 %all-to-all-start = ((f32[16,72,128]{2,1,0:T(8,128)}), f32[16,72,128]{2,1,0:T(8,128)S(1)}, u32[]{:S(2)}, u32[]{:S(2)}) async-start(f32[16,72,128]{2,1,0:T(8,128)} %get-tuple-element.22), calls=%async_computation | async-start | bytes 1179648 | tf_op jit(solution)/shard_map/all_to_all | solution.py:496
  42.3 0.0 copy-start.5
  42.3 0.0 copy-done.6
  42.3 0.1 dynamic_slice.6
  42.3 0.6 copy-done.5
  42.9 0.1 broadcast_add_fusion.mu
  43.0 9.8 %all-to-all-done.recv = f32[16,72,128]{2,1,0:T(8,128)S(1)} async-done(((f32[16,72,128]{2,1,0:T(8,128)}), f32[16,72,128]{2,1,0:T(8,128)S(1)}, u32[]{:S(2)}, u32[]{:S(2)}) %all-to-all-start) | async-done | bytes 589856 | tf_op jit(solution)/shard_map/all_to_all | solution.py:496
  52.8 0.0 copy-done
  52.8 0.0 copy-done.1
  52.8 1.7 %transform.1 = (f32[272,512]{1,0:T(8,128)S(1)}, f32[32,4,128]{2,1,0:T(4,128)}) custom-call(f32[16,72,128]{2,1,0:T(8,128)S(1)} %all-to-all-done.recv, f32[16,512]{1,0:T(8,128)S(1)} %broadcast_add_fusion.mu, bf16[384,512]{1,0:T(8,128)(2,1)S(1)} %copy-done.1, bf16[384,512]{1,0:T(8,128)(2,1)S(1)} %copy-done), custom_call_target="tpu_custom_call" | custom-call | tf_op jit(solution)/shard_map/transform/pallas_call | solution.py:286
  54.5 7.0 %all-to-all-start.1 = ((f32[32,4,128]{2,1,0:T(4,128)}), f32[32,4,128]{2,1,0:T(4,128)S(1)}, u32[]{:S(2)}, u32[]{:S(2)}) async-start(f32[32,4,128]{2,1,0:T(4,128)} %get-tuple-element.24), calls=%async_computation.1 | async-start | bytes 131072 | tf_op jit(solution)/shard_map/all_to_all | solution.py:497
  61.5 0.1 dynamic_slice.7.mu
  61.6 11.2 %all-to-all-done.1.sums = f32[32,4,128]{2,1,0:T(4,128)S(1)} async-done(((f32[32,4,128]{2,1,0:T(4,128)}), f32[32,4,128]{2,1,0:T(4,128)S(1)}, u32[]{:S(2)}, u32[]{:S(2)}) %all-to-all-start.1) | async-done | bytes 65568 | tf_op jit(solution)/shard_map/all_to_all | solution.py:497
  72.8 0.0 copy-start.4
  72.8 0.8 carry.1
  73.6 15.1 %all_to_all.20.carries = f32[32,4,128]{2,1,0:T(4,128)S(1)} all-to-all(f32[32,4,128]{2,1,0:T(4,128)} %carry.1), channel_id=1, replica_groups=mesh['aisle'=32,'span'=16] {'aisle'}, dimensions={0} | all-to-all | bytes 131072 | tf_op jit(solution)/shard_map/all_to_all | solution.py:498
  88.7 0.0 copy-done.4
  88.7 1.9 %inverse.1 = f32[16,72,128]{2,1,0:T(8,128)} custom-call(f32[272,512]{1,0:T(8,128)S(1)} %get-tuple-element.23.local, f32[32,4,128]{2,1,0:T(4,128)S(1)} %all_to_all.20.carries, f32[16,512]{1,0:T(8,128)S(1)} %broadcast_add_fusion.mu, f32[1,512]{1,0:T(1,128)S(1)} %copy-done.4, bf16[384,512]{1,0:T(8,128)(2,1)S(1)} %copy-done.1, bf16[384,512]{1,0:T(8,128)(2,1)S(1)} %copy-done), custom_call_target="tpu_custom_call" | custom-call | tf_op jit(solution)/shard_map/inverse/pallas_call | solution.py:392
  90.7 0.0 copy-start.2
  90.7 18.6 %all_to_all.21.recv = f32[16,72,128]{2,1,0:T(8,128)S(1)} all-to-all(f32[16,72,128]{2,1,0:T(8,128)} %inverse.1), channel_id=1, replica_groups=mesh['aisle'=32,'span'=16] {'span'}, dimensions={0} | all-to-all | bytes 1179648 | tf_op jit(solution)/shard_map/all_to_all | solution.py:499
  109.2 0.0 copy-done.2
  109.2 3.9 %correct.1 = (f32[16,32,256]{2,1,0:T(8,128)}, f32[16,32,256]{2,1,0:T(8,128)}, f32[16,32,256]{2,1,0:T(8,128)}) custom-call(f32[16,72,128]{2,1,0:T(8,128)S(1)} %all_to_all.21.recv, f32[256,256]{1,0:T(8,128)S(1)} %copy-done.2, f32[16,32,256]{2,1,0:T(8,128)} %get-tuple-element.25.es, f32[16,32,256]{2,1,0:T(8,128)} %get-tuple-element.26.ns, ...), custom_call_target="tpu_custom_call" | custom-call | tf_op jit(solution)/shard_map/correct/pallas_call | solution.py:453
Async XLA Ops:
  0.6 28.3 %copy-start.3 = (f32[256,256]{1,0:T(8,128)S(1)}, f32[256,256]{1,0:T(8,128)}, u32[]{:S(2)}) copy-start(f32[256,256]{1,0:T(8,128)} %basis.2) | copy-start | bytes 786436
  2.8 26.1 %collective-permute-start = (f32[4,32,256]{2,1,0:T(8,128)}, f32[4,32,256]{2,1,0:T(8,128)S(1)}, u32[]{:S(2)}, u32[]{:S(2)}) collective-permute-start(f32[4,32,256]{2,1,0:T(8,128)} %get-tuple-element.18), channel_id=1, source_target_pairs={{0,16},{16,32},{32,48},{48,64},{64,80},{80,96},{96,112},{112,128},... | collective-permute-start | bytes 393224 | tf_op jit(solution)/shard_map/ppermute | solution.py:469
  6.9 22.0 %collective-permute-start.1 = (f32[4,32,256]{2,1,0:T(8,128)}, f32[4,32,256]{2,1,0:T(8,128)S(1)}, u32[]{:S(2)}, u32[]{:S(2)}) collective-permute-start(f32[4,32,256]{2,1,0:T(8,128)} %get-tuple-element.19), channel_id=1, source_target_pairs={{0,496},{16,0},{32,16},{48,32},{64,48},{80,64},{96,80},{112,96},{1... | collective-permute-start | bytes 393224 | tf_op jit(solution)/shard_map/ppermute | solution.py:469
  19.1 5.9 %collective-permute-start.2 = (f32[4,16,256]{2,1,0:T(8,128)}, f32[4,16,256]{2,1,0:T(8,128)S(1)}, u32[]{:S(2)}, u32[]{:S(2)}) collective-permute-start(f32[4,16,256]{2,1,0:T(8,128)} %get-tuple-element.20), channel_id=1, source_target_pairs={{0,1},{1,2},{2,3},{3,4},{4,5},{5,6},{6,7},{7,8},{8,9},{9,10},{10,1... | collective-permute-start | bytes 196616 | tf_op jit(solution)/shard_map/ppermute | solution.py:469
  23.1 5.8 %collective-permute-start.3 = (f32[4,16,256]{2,1,0:T(8,128)}, f32[4,16,256]{2,1,0:T(8,128)S(1)}, u32[]{:S(2)}, u32[]{:S(2)}) collective-permute-start(f32[4,16,256]{2,1,0:T(8,128)} %get-tuple-element.21), channel_id=1, source_target_pairs={{0,15},{1,0},{2,1},{3,2},{4,3},{5,4},{6,5},{7,6},{8,7},{9,8},{10,9... | collective-permute-start | bytes 196616 | tf_op jit(solution)/shard_map/ppermute | solution.py:469
  35.9 6.4 %copy-start.6 = (f32[256]{0:T(256)S(1)}, f32[256]{0:T(256)}, u32[]{:S(2)}) copy-start(f32[256]{0:T(256)} %param.17) | copy-start | bytes 3076
  35.9 16.9 %copy-start = (bf16[384,512]{1,0:T(8,128)(2,1)S(1)}, bf16[384,512]{1,0:T(8,128)(2,1)}, u32[]{:S(2)}) copy-start(bf16[384,512]{1,0:T(8,128)(2,1)} %constant.67.clone.low) | copy-start | bytes 1179652
  35.9 16.9 %copy-start.1 = (bf16[384,512]{1,0:T(8,128)(2,1)S(1)}, bf16[384,512]{1,0:T(8,128)(2,1)}, u32[]{:S(2)}) copy-start(bf16[384,512]{1,0:T(8,128)(2,1)} %constant.66.clone.high) | copy-start | bytes 1179652
  35.9 16.9 %all-to-all-start = ((f32[16,72,128]{2,1,0:T(8,128)}), f32[16,72,128]{2,1,0:T(8,128)S(1)}, u32[]{:S(2)}, u32[]{:S(2)}) async-start(f32[16,72,128]{2,1,0:T(8,128)} %get-tuple-element.22), calls=%async_computation | async-start | bytes 1179648 | tf_op jit(solution)/shard_map/all_to_all | solution.py:496
  42.3 0.7 copy-start.5
  54.5 18.3 %all-to-all-start.1 = ((f32[32,4,128]{2,1,0:T(4,128)}), f32[32,4,128]{2,1,0:T(4,128)S(1)}, u32[]{:S(2)}, u32[]{:S(2)}) async-start(f32[32,4,128]{2,1,0:T(4,128)} %get-tuple-element.24), calls=%async_computation.1 | async-start | bytes 131072 | tf_op jit(solution)/shard_map/all_to_all | solution.py:497
  72.8 15.9 %copy-start.4 = (f32[1,512]{1,0:T(1,128)S(1)}, f32[1,512]{1,0:T(1,128)}, u32[]{:S(2)}) copy-start(f32[1,512]{1,0:T(1,128)} %constant.73.weight) | copy-start | bytes 6148
  90.7 18.6 %copy-start.2 = (f32[256,256]{1,0:T(8,128)S(1)}, f32[256,256]{1,0:T(8,128)}, u32[]{:S(2)}) copy-start(f32[256,256]{1,0:T(8,128)} %basis.3) | copy-start | bytes 786436
